TPU v7x, 32 devices: a whole 2x2x4 slice. The times are simulated.
32 devices in a mesh: dp: 2 (over y), fsdp: 16 (over z, x, core).
Axes of the slice: x: 2, y: 2, z: 4, core: 2. Of those that a mesh axis runs over, the one named last changes fastest.
Arguments:
- ids: int32 [2, 192], P('dp'), may hold values from 0 to 511
- embed: bfloat16 [512, 8192], P(None, 'fsdp'), may hold values from -32 to 32
- gain: bfloat16 [8192], P('fsdp'), may hold values from 0.099609375 to 1.8984375
- w_in: bfloat16 [3, 4096, 8192], P(None, 'fsdp'), may hold values from -0.0625 to 0.0625
- feat_filter: float32 [3, 256, 7], P(None, 'fsdp'), may hold values from -2.4 to 2.4
- inner_filter: float32 [256, 7], P('fsdp'), may hold values from -2.4 to 2.4
- w_out: bfloat16 [4096, 8192], P(None, 'fsdp'), may hold values from -0.09375 to 0.09375
- cotangent: bfloat16 [2, 192, 8192], P('dp', None, 'fsdp'), may hold values from -6 to 6
- right_prev: bfloat16 [8192, 256], P('fsdp'), may hold values from -6 to 6
Outputs:
- block_out: bfloat16 [2, 192, 8192], P('dp', None, 'fsdp')
- filter_grad: float32 [4, 256, 7], P(None, 'fsdp')
- basis: bfloat16 [4096, 256], P('fsdp')
- right_factor: float32 [8192, 256], P('fsdp')
All inputs are finite; a program needn't handle non-finite values.
Results may differ from a plain program's by a relative error of at most 0.014.
The roundings to bfloat16 on the way count: a program that leaves them out, or rounds other values in their place, can miss the bound.
Values may be sent and summed in bfloat16 or wider, within the bound.
No kernel may reach another device: no remote copies, remote signals or barrier semaphores. Data moves between devices by JAX's collectives and lax.ppermute only.
A program may use at most 128 MiB of HBM per device.

v0:
```python
import jax
import jax.numpy as jnp
from jax import lax
from jax.sharding import PartitionSpec as P

D = 8192
C = 4096
GROUP = 16


def shifted(signal, lag, tap_count):
    padded = jnp.pad(signal, ((tap_count - 1, 0), (0, 0)))
    first = tap_count - 1 - lag
    return padded[first : first + signal.shape[0]]


def causal(signal, tap_table):
    tap_count = tap_table.shape[0]
    result = jnp.zeros(signal.shape, jnp.float32)
    for lag in range(tap_count):
        result = result + tap_table[lag][None, :] * shifted(signal, lag, tap_count)
    return result


def anticausal(signal, tap_table):
    tap_count = tap_table.shape[0]
    padded = jnp.pad(signal, ((0, tap_count - 1), (0, 0)))
    result = jnp.zeros(signal.shape, jnp.float32)
    for lag in range(tap_count):
        result = result + tap_table[lag][None, :] * padded[lag : lag + signal.shape[0]]
    return result


def tap_sums(gradient, signal, tap_count):
    listing = []
    for lag in range(tap_count):
        listing.append(jnp.sum(gradient * shifted(signal, lag, tap_count), axis=0))
    stacked = jnp.stack(listing, axis=0)
    grouped = stacked.reshape(tap_count, stacked.shape[1] // GROUP, GROUP).sum(axis=2)
    return grouped.T


def expand(filters):
    return jnp.repeat(filters.T, GROUP, axis=1)


def per_device(ids, embed, gain, w_in, feat_filter, inner_filter, w_out, cotangent, right_prev):
    tokens = ids[0]
    length = tokens.shape[0]
    tap_count = inner_filter.shape[1]
    onehot = (tokens[:, None] == jnp.arange(embed.shape[0], dtype=jnp.int32)[None, :]).astype(
        jnp.bfloat16
    )
    x_cols = jnp.dot(onehot, embed, preferred_element_type=jnp.float32)
    square_sums = lax.psum(jnp.sum(x_cols * x_cols, axis=1), "fsdp")
    factor = lax.rsqrt(square_sums / D + 1e-05)
    normed_cols = (x_cols * factor[:, None] * gain.astype(jnp.float32)[None, :]).astype(
        jnp.bfloat16
    )
    projected = jnp.einsum(
        "ld,kcd->klc",
        lax.all_gather(normed_cols, "fsdp", axis=1, tiled=True),
        w_in,
        preferred_element_type=jnp.float32,
    )
    rounded = lax.optimization_barrier(projected.astype(jnp.bfloat16)).astype(jnp.float32)
    query, key_in, value = (rounded[0], rounded[1], rounded[2])
    query_conv = causal(query, expand(feat_filter[0]))
    key_conv = causal(key_in, expand(feat_filter[1]))
    value_conv = causal(value, expand(feat_filter[2]))
    gated = key_conv * value_conv
    inner_table = expand(inner_filter)
    window = causal(gated, inner_table)
    gated_out = (query_conv * window).astype(jnp.bfloat16)
    cot_cols = cotangent[0]
    shard_piece = lax.all_gather(gated_out, "fsdp", axis=1, tiled=True)
    weight_rows = w_out
    mixed_sum = jnp.dot(shard_piece, weight_rows, preferred_element_type=jnp.float32)
    term = jnp.einsum("lc,ld->cd", shard_piece, cot_cols, preferred_element_type=jnp.float32)
    mixed_sum, grad_part = (mixed_sum, term)
    block_out = (x_cols + mixed_sum).astype(jnp.bfloat16)[None]
    weight_rows = w_out
    mixed_grad = lax.psum_scatter(
        jnp.einsum("cd,ld->cl", weight_rows, cot_cols, preferred_element_type=jnp.float32),
        "fsdp",
        scatter_dimension=0,
        tiled=True,
    ).T
    query_grad = mixed_grad * window
    window_grad = mixed_grad * query_conv
    gated_grad = anticausal(window_grad, inner_table)
    key_grad = gated_grad * value_conv
    value_grad = gated_grad * key_conv
    norm_factor = 1.0 / jnp.sqrt(jnp.float32(lax.axis_size("dp") * length))
    filter_part = (
        jnp.stack(
            [
                tap_sums(query_grad, query, tap_count),
                tap_sums(key_grad, key_in, tap_count),
                tap_sums(value_grad, value, tap_count),
                tap_sums(window_grad, gated, tap_count),
            ],
            axis=0,
        )
        * norm_factor
    )
    grad_total, filter_grad = (
        lax.psum(grad_part.astype(jnp.bfloat16), "dp").astype(jnp.float32),
        lax.psum(filter_part.astype(jnp.bfloat16), "dp").astype(jnp.float32),
    )
    grad_half = grad_total.astype(jnp.bfloat16)
    grad_rows_own = lax.all_to_all(grad_half, "fsdp", split_axis=0, concat_axis=1, tiled=True)
    panel_own = jnp.dot(
        grad_rows_own,
        lax.all_gather(right_prev, "fsdp", axis=0, tiled=True),
        preferred_element_type=jnp.float32,
    ).astype(jnp.bfloat16)
    root_scale = jnp.sqrt(jnp.float32(C))
    gram_local = jnp.einsum("cr,cs->rs", panel_own, panel_own, preferred_element_type=jnp.float32)
    gram_matrix = lax.psum(gram_local, "fsdp")
    lower_factor = jnp.linalg.cholesky(gram_matrix)
    solved = jax.scipy.linalg.solve_triangular(
        lower_factor, panel_own.astype(jnp.float32).T, lower=True
    ).T
    basis_own = (solved * root_scale).astype(jnp.bfloat16)
    right_raw = jnp.einsum(
        "cd,cr->dr",
        grad_half,
        lax.all_gather(basis_own, "fsdp", axis=0, tiled=True),
        preferred_element_type=jnp.float32,
    )
    column_sums = lax.psum(jnp.sum(right_raw * right_raw, axis=0), "fsdp")
    right_factor = right_raw * lax.rsqrt(column_sums / D + 1e-06)[None, :]
    return (block_out, filter_grad, basis_own, right_factor)


def solution(mesh):
    placed = (
        P("dp", None),
        P(None, "fsdp"),
        P("fsdp"),
        P(None, "fsdp", None),
        P(None, "fsdp", None),
        P("fsdp", None),
        P(None, "fsdp"),
        P("dp", None, "fsdp"),
        P("fsdp", None),
    )
    return jax.shard_map(
        per_device,
        mesh=mesh,
        in_specs=placed,
        out_specs=(P("dp", None, "fsdp"), P(None, "fsdp", None), P("fsdp", None), P("fsdp", None)),
        check_vma=False,
    )
```

profile of v0, /device:TPU:0, one launch (start us, length us, event | category | flops | bytes accessed | tf_op | source)
XLA Modules:
  0.0 699.4 jit_solution(17935779332028869934)
XLA Ops:
  9.3 34.9 %psum.35 = f32[192]{0:T(256)S(1)} all-reduce(f32[192]{0:T(256)S(1)} %get-tuple-element.121), channel_id=1, replica_groups=mesh['dp'=2,'fsdp'=16] {'fsdp'}, use_global_device_ids=true, to_apply=%region_1.0 | all-reduce | flops 192 | bytes 1536 | tf_op jit(solution)/shard_map/psum | solution.py:55
  45.1 5.4 fusion.14
  55.0 34.7 %all-gather.5.cloned.1.call-done = bf16[192,8192]{1,0:T(8,128)(2,1)} async-done(((bf16[192,512]{1,0:T(8,128)(2,1)}), bf16[192,8192]{1,0:T(8,128)(2,1)}) %all-gather.5.cloned.1.call-update) | async-done | bytes 3145744 | tf_op jit(solution)/shard_map/all_gather | solution.py:62
  89.7 9.8 %fusion.6 = bf16[3,192,256]{2,1,0:T(8,128)(2,1)S(1)} fusion(bf16[3,256,8192]{2,1,0:T(8,128)(2,1)} %param.12, bf16[192,8192]{1,0:T(8,128)(2,1)} %all-gather.5.cloned.1.call-done), kind=kOutput, calls=%fused_computation.8 | convolution fusion | flops 2416066560 | bytes 16023552 | tf_op jit(solution)/shard_map/ld,kcd->klc/dot_general | solution.py:60
  99.6 58.3 %reduce-scatter.2.cloned.1.call-done = f32[256,192]{0,1:T(8,128)} async-done(((f32[4096,192]{0,1:T(8,128)}), f32[256,192]{0,1:T(8,128)}) %reduce-scatter.2.cloned.1.call-update) | async-done | bytes 196624 | tf_op jit(solution)/shard_map/reduce_scatter | solution.py:83
  161.0 2.6 multiply_reduce_fusion.23
  164.3 38.0 %all-gather.7.cloned.1.call-done = bf16[192,4096]{1,0:T(8,128)(2,1)} async-done(((bf16[192,256]{1,0:T(8,128)(2,1)}), bf16[192,4096]{1,0:T(8,128)(2,1)}) %all-gather.7.cloned.1.call-update) | async-done | bytes 1572880 | tf_op jit(solution)/shard_map/all_gather | solution.py:76
  202.3 4.7 convolution_convert_fusion
  207.7 106.5 %all-reduce.9.cloned.1.call-done = bf16[4096,512]{1,0:T(8,128)(2,1)} async-done(((bf16[4096,512]{1,0:T(8,128)(2,1)}), bf16[4096,512]{1,0:T(8,128)(2,1)}) %all-reduce.9.cloned.1.call-update) | async-done | bytes 4194320 | tf_op jit(solution)/shard_map/psum | solution.py:108
  314.2 6.4 copy.22
  320.6 5.7 all-to-all-start
  326.3 94.7 %all-gather.9.cloned.1.call-done = bf16[8192,256]{1,0:T(8,128)(2,1)} async-done(((bf16[512,256]{1,0:T(8,128)(2,1)}), bf16[8192,256]{1,0:T(8,128)(2,1)}) %all-gather.9.cloned.1.call-update) | async-done | bytes 4194320 | tf_op jit(solution)/shard_map/all_gather | solution.py:115
  421.0 6.5 all-to-all-done
  427.4 4.8 convolution_convert_fusion.1
  434.0 103.0 %all-reduce.11.cloned.1.call-done = f32[256,256]{0,1:T(8,128)} async-done(((f32[256,256]{0,1:T(8,128)}), f32[256,256]{0,1:T(8,128)}) %all-reduce.11.cloned.1.call-update) | async-done | bytes 262160 | tf_op jit(solution)/shard_map/psum | solution.py:120
  537.0 1.8 copy.24
  540.6 11.7 %cholesky.50 = f32[128,128]{1,0:T(8,128)S(1)} custom-call(f32[128,128]{1,0:T(8,128)S(1)} %cholesky.118), custom_call_target="Cholesky" | custom-call | tf_op jit(solution)/shard_map/jit(cholesky)/cholesky | solution.py:121
  553.6 9.8 %custom-call.15 = f32[1,128,128]{1,2,0:T(8,128)S(1)} custom-call(f32[1,128,128]{2,1,0:T(8,128)S(1)} %get-tuple-element.89), custom_call_target="InvertDiagBlocksLowerTriangular" | custom-call | tf_op jit(solution)/shard_map/jit(cholesky)/cholesky | solution.py:121
  563.4 1.7 constant_dynamic-update-slice_fusion.29
  566.2 11.7 %cholesky.105 = f32[128,128]{1,0:T(8,128)S(1)} custom-call(f32[128,128]{1,0:T(8,128)S(1)} %convolution_subtract_fusion.1), custom_call_target="Cholesky" | custom-call | tf_op jit(solution)/shard_map/jit(cholesky)/cholesky | solution.py:121
  581.7 1.7 select_select_fusion
  584.2 6.8 while.1
  584.8 2.9 bitcast_dynamic-update-slice_fusion.2
  588.2 2.8 bitcast_dynamic-update-slice_fusion.2
  591.0 20.5 %custom-call.16 = f32[2,128,128]{1,2,0:T(8,128)S(1)} custom-call(f32[2,128,128]{2,1,0:T(8,128)} %get-tuple-element.11), custom_call_target="InvertDiagBlocksLowerTriangular" | custom-call | tf_op jit(solution)/shard_map/jit(_solve_triangular)/triangular_solve | solution.py:122
  614.0 1.9 multiply_reduce_fusion.2
  616.6 2.0 multiply_reduce_fusion.29
  622.1 5.0 psum.36
  627.8 3.8 fusion.9
  632.4 23.5 %all-gather.11.cloned.1.call-done = bf16[4096,256]{0,1:T(8,128)(2,1)} async-done(((bf16[256,256]{0,1:T(8,128)(2,1)}), bf16[4096,256]{0,1:T(8,128)(2,1)}) %all-gather.11.cloned.1.call-update) | async-done | bytes 2097168 | tf_op jit(solution)/shard_map/all_gather | solution.py:129
  655.9 4.2 multiply_reduce_fusion
  660.1 31.6 %psum.39 = f32[256]{0:T(256)S(1)} all-reduce(f32[256]{0:T(256)S(1)} %get-tuple-element.125), channel_id=1, replica_groups=mesh['dp'=2,'fsdp'=16] {'fsdp'}, use_global_device_ids=true, to_apply=%region_43.44 | all-reduce | flops 256 | bytes 2048 | tf_op jit(solution)/shard_map/psum | solution.py:132
  (190 shorter events, 31.1 us)
Async XLA Ops:
  7.2 1.1 copy-start
  7.2 82.5 %all-gather.5.cloned.1.call-start = ((), (), s32[]{:S(2)}) async-start(), calls=%async_computation.2 | async-start | bytes 3342336 | tf_op jit(solution)/shard_map/all_gather | solution.py:62
  45.0 5.5 copy-start.8
  45.0 6.6 copy-start.9
  45.1 112.9 %reduce-scatter.2.cloned.1.call-start = ((), (), s32[]{:S(2)}) async-start(), calls=%async_computation.4 | async-start | bytes 3342336 | tf_op jit(solution)/shard_map/reduce_scatter | solution.py:83
  50.5 151.8 %all-gather.7.cloned.1.call-start = ((), (), s32[]{:S(2)}) async-start(), calls=%async_computation.3 | async-start | bytes 1671168 | tf_op jit(solution)/shard_map/all_gather | solution.py:76
  99.5 102.8 %copy-start.7 = (bf16[1,192,512]{2,1,0:T(8,128)(2,1)S(1)}, bf16[1,192,512]{2,1,0:T(8,128)(2,1)}, u32[]{:S(2)}) copy-start(bf16[1,192,512]{2,1,0:T(8,128)(2,1)} %param.16) | copy-start | bytes 589828
  99.6 61.3 %copy-start.3 = (f32[192,256]{1,0:T(8,128)}, f32[192,256]{1,0:T(8,128)S(1)}, u32[]{:S(2)}) copy-start(f32[192,256]{1,0:T(8,128)S(1)} %get-tuple-element.84) | copy-start | bytes 589828
  159.1 48.0 %copy-start.4 = (f32[192,256]{1,0:T(8,128)}, f32[192,256]{1,0:T(8,128)S(1)}, u32[]{:S(2)}) copy-start(f32[192,256]{1,0:T(8,128)S(1)} %get-tuple-element.79) | copy-start | bytes 589828
  161.0 46.1 %copy-start.2 = (f32[192,256]{1,0:T(8,128)}, f32[192,256]{1,0:T(8,128)S(1)}, u32[]{:S(2)}) copy-start(f32[192,256]{1,0:T(8,128)S(1)} %mul.459) | copy-start | bytes 589828
  164.2 150.0 %all-reduce.9.cloned.1.call-start = ((), (), s32[]{:S(2)}) async-start(), calls=%async_computation.5 | async-start | bytes 8388608 | tf_op jit(solution)/shard_map/psum | solution.py:108
  207.1 213.9 %all-gather.9.cloned.1.call-start = ((), (), s32[]{:S(2)}) async-start(), calls=%async_computation.6 | async-start | bytes 4456448 | tf_op jit(solution)/shard_map/all_gather | solution.py:115
  320.6 106.8 %all-to-all-start = ((bf16[16,256,512]{1,2,0:T(8,128)(2,1)}), bf16[16,256,512]{1,2,0:T(8,128)(2,1)}, u32[]{:S(2)}, u32[]{:S(2)}) async-start(bf16[16,256,512]{1,2,0:T(8,128)(2,1)} %copy.22), calls=%async_computation.1 | async-start | bytes 8388608 | tf_op jit(solution)/shard_map/all_to_all | solution.py:112
  326.2 210.8 %all-reduce.11.cloned.1.call-start = ((), (), s32[]{:S(2)}) async-start(), calls=%async_computation.7 | async-start | bytes 524288 | tf_op jit(solution)/shard_map/psum | solution.py:120
  433.2 222.7 %all-gather.11.cloned.1.call-start = ((), (), s32[]{:S(2)}) async-start(), calls=%async_computation.8 | async-start | bytes 2228224 | tf_op jit(solution)/shard_map/all_gather | solution.py:129
  434.0 193.8 %copy-start.1 = (bf16[192,4096]{1,0:T(8,128)(2,1)S(1)}, bf16[192,4096]{1,0:T(8,128)(2,1)}, u32[]{:S(2)}) copy-start(bf16[192,4096]{1,0:T(8,128)(2,1)} %all-gather.7.cloned.1.call-done) | copy-start | bytes 4718596
  539.9 0.7 copy-start.6
  616.6 15.0 %copy-start.5 = (bf16[256,256]{0,1:T(8,128)(2,1)S(1)}, bf16[256,256]{0,1:T(8,128)(2,1)}, u32[]{:S(2)}) copy-start(bf16[256,256]{0,1:T(8,128)(2,1)} %fusion.19) | copy-start | bytes 393220
Sparse Core Ops, SparseCore 0:
  45.2 44.4 all-gather.4
  93.5 64.4 reduce-scatter.1
  164.4 37.9 all-gather.6
  207.2 106.9 all-reduce.8
  316.4 104.4 all-gather.8
  433.3 103.7 all-reduce.10
  614.1 41.7 all-gather.10
where the time goes:
time: 700 us; the launch traced here: 699 us
  waiting for transfers between devices  466 us (67%)
  other arithmetic  73.8 us (11%)
  blocking collectives  71.5 us (10%)
  matrix products  39.3 us (6%)
  local copies, waits for them, and re-layouts  26.9 us (4%)
  between operations  15.8 us (2%)
    psum x1, waiting for transfers between devices, per_device(): lax.psum(grad_part.astype(jnp.bfloat16), 'dp').astype(jnp.float32)  107 us
    psum x1, waiting for transfers between devices, per_device(): gram_matrix = lax.psum(gram_local, 'fsdp')  103 us
    all_gather x1, waiting for transfers between devices, per_device(): lax.all_gather(right_prev, 'fsdp', axis=0, tiled=True)  94.7 us
    reduce_scatter x1, waiting for transfers between devices, per_device(): lax.psum_scatter(jnp.einsum('cd,ld->cl', weight_rows, cot_cols, preferred...  58.3 us
    all_gather x1, waiting for transfers between devices, per_device(): shard_piece = lax.all_gather(gated_out, 'fsdp', axis=1, tiled=True)  38 us
    another operation x7, other arithmetic, per_device(): lower_factor = jnp.linalg.cholesky(gram_matrix)  36.4 us
    psum x1, blocking collectives, per_device(): square_sums = lax.psum(jnp.sum(x_cols * x_cols, axis=1), 'fsdp')  34.9 us
    all_gather x1, waiting for transfers between devices, per_device(): lax.all_gather(normed_cols, 'fsdp', axis=1, tiled=True)  34.7 us
  transfers between devices with their start and end apart: 8, of which 8 were waited for; matrix products, arithmetic and copies ran while one was open for 6% of the time, Pallas kernels for 0%

commit v1 on v0

--- a/solution.py
+++ b/solution.py
@@ -123,12 +123,37 @@
         lower_factor, panel_own.astype(jnp.float32).T, lower=True
     ).T
     basis_own = (solved * root_scale).astype(jnp.bfloat16)
+    count, index, span = (lax.axis_size("fsdp"), lax.axis_index("fsdp"), basis_own.shape[0])
+    forward = [(i, (i + 1) % count) for i in range(count)]
+    backward = [(i, (i - 1) % count) for i in range(count)]
+    middle = count // 2
+    from_left = from_right = basis_own
     right_raw = jnp.einsum(
         "cd,cr->dr",
-        grad_half,
-        lax.all_gather(basis_own, "fsdp", axis=0, tiled=True),
+        lax.dynamic_slice_in_dim(grad_half, index * span, basis_own.shape[0], axis=0),
+        basis_own,
         preferred_element_type=jnp.float32,
     )
+    for step in range(1, middle + 1):
+        from_left = lax.ppermute(from_left, "fsdp", forward)
+        if step < count - middle:
+            from_right = lax.ppermute(from_right, "fsdp", backward)
+            right_raw = right_raw + jnp.einsum(
+                "cd,cr->dr",
+                lax.dynamic_slice_in_dim(
+                    grad_half, (index + step) % count * span, from_right.shape[0], axis=0
+                ),
+                from_right,
+                preferred_element_type=jnp.float32,
+            )
+        right_raw = right_raw + jnp.einsum(
+            "cd,cr->dr",
+            lax.dynamic_slice_in_dim(
+                grad_half, (index - step) % count * span, from_left.shape[0], axis=0
+            ),
+            from_left,
+            preferred_element_type=jnp.float32,
+        )
     column_sums = lax.psum(jnp.sum(right_raw * right_raw, axis=0), "fsdp")
     right_factor = right_raw * lax.rsqrt(column_sums / D + 1e-06)[None, :]
     return (block_out, filter_grad, basis_own, right_factor)

time: 700 us -> 699 us (level)
  starting transfers between devices: 6.13 us -> 38.1 us
  waiting for transfers between devices: 466 us -> 449 us
  other arithmetic: 73.8 us -> 63.1 us
    ppermute x0 -> x15, starting transfers between devices: none -> 32.2 us  [the longest x7 31.5 us: per_device(): from_right = lax.ppermute(from_right, 'fsdp', backward)]
    all_gather x1 -> x0, waiting for transfers between devices: 23.5 us -> none  [per_device(): lax.all_gather(basis_own, 'fsdp', axis=0, tiled=True)]
    ppermute x0 -> x15, waiting for transfers between devices: none -> 15.7 us  [the longest x8 11.7 us: per_device(): from_left = lax.ppermute(from_left, 'fsdp', forward)]
  transfers between devices with their start and end apart: 8 -> 22, of which waited for: 8 -> 19; matrix products, arithmetic and copies ran while one was open for 6% -> 6% of each run, Pallas kernels for 0% -> 0%
where the time goes in v1:
time: 699 us; the launch traced here: 698 us
  waiting for transfers between devices  449 us (64%)
  blocking collectives  69.4 us (10%)
  other arithmetic  63.1 us (9%)
  matrix products  40.3 us (6%)
  starting transfers between devices  38.1 us (5%)
  local copies, waits for them, and re-layouts  21 us (3%)
  between operations  16.4 us (2%)
    psum x1, waiting for transfers between devices, per_device(): lax.psum(grad_part.astype(jnp.bfloat16), 'dp').astype(jnp.float32)  107 us
    psum x1, waiting for transfers between devices, per_device(): gram_matrix = lax.psum(gram_local, 'fsdp')  97.8 us
    all_gather x1, waiting for transfers between devices, per_device(): lax.all_gather(right_prev, 'fsdp', axis=0, tiled=True)  91.2 us
    reduce_scatter x1, waiting for transfers between devices, per_device(): lax.psum_scatter(jnp.einsum('cd,ld->cl', weight_rows, cot_cols, preferred...  58.4 us
    all_gather x1, waiting for transfers between devices, per_device(): shard_piece = lax.all_gather(gated_out, 'fsdp', axis=1, tiled=True)  38.1 us
    psum x1, blocking collectives, per_device(): square_sums = lax.psum(jnp.sum(x_cols * x_cols, axis=1), 'fsdp')  34.9 us
    all_gather x1, waiting for transfers between devices, per_device(): lax.all_gather(normed_cols, 'fsdp', axis=1, tiled=True)  34.7 us
    another operation x7, other arithmetic, per_device(): lower_factor = jnp.linalg.cholesky(gram_matrix)  34.6 us
  transfers between devices with their start and end apart: 22, of which 19 were waited for; matrix products, arithmetic and copies ran while one was open for 6% of the time, Pallas kernels for 0%

profile of v1, /device:TPU:0, one launch (start us, length us, event | category | flops | bytes accessed | tf_op | source)
XLA Modules:
  0.0 697.9 jit_solution(12297528225318314122)
XLA Ops:
  9.3 34.9 %psum.35 = f32[192]{0:T(256)S(1)} all-reduce(f32[192]{0:T(256)S(1)} %get-tuple-element.121), channel_id=1, replica_groups=mesh['dp'=2,'fsdp'=16] {'fsdp'}, use_global_device_ids=true, to_apply=%region_1.0 | all-reduce | flops 192 | bytes 1536 | tf_op jit(solution)/shard_map/psum | solution.py:55
  45.1 5.4 fusion.43
  55.0 34.7 %all-gather.4.cloned.1.call-done = bf16[192,8192]{1,0:T(8,128)(2,1)} async-done(((bf16[192,512]{1,0:T(8,128)(2,1)}), bf16[192,8192]{1,0:T(8,128)(2,1)}) %all-gather.4.cloned.1.call-update) | async-done | bytes 3145744 | tf_op jit(solution)/shard_map/all_gather | solution.py:62
  89.7 9.8 %fusion.12 = bf16[3,192,256]{2,1,0:T(8,128)(2,1)S(1)} fusion(bf16[3,256,8192]{2,1,0:T(8,128)(2,1)} %param.12, bf16[192,8192]{1,0:T(8,128)(2,1)} %all-gather.4.cloned.1.call-done), kind=kOutput, calls=%fused_computation.23 | convolution fusion | flops 2416066560 | bytes 16023552 | tf_op jit(solution)/shard_map/ld,kcd->klc/dot_general | solution.py:60
  99.6 58.4 %reduce-scatter.2.cloned.1.call-done = f32[256,192]{0,1:T(8,128)} async-done(((f32[4096,192]{0,1:T(8,128)}), f32[256,192]{0,1:T(8,128)}) %reduce-scatter.2.cloned.1.call-update) | async-done | bytes 196624 | tf_op jit(solution)/shard_map/reduce_scatter | solution.py:83
  161.6 38.1 %all-gather.6.cloned.1.call-done = bf16[192,4096]{1,0:T(8,128)(2,1)} async-done(((bf16[192,256]{1,0:T(8,128)(2,1)}), bf16[192,4096]{1,0:T(8,128)(2,1)}) %all-gather.6.cloned.1.call-update) | async-done | bytes 1572880 | tf_op jit(solution)/shard_map/all_gather | solution.py:76
  199.7 4.7 convolution_convert_fusion
  205.0 106.5 %all-reduce.9.cloned.1.call-done = bf16[4096,512]{1,0:T(8,128)(2,1)} async-done(((bf16[4096,512]{1,0:T(8,128)(2,1)}), bf16[4096,512]{1,0:T(8,128)(2,1)}) %all-reduce.9.cloned.1.call-update) | async-done | bytes 4194320 | tf_op jit(solution)/shard_map/psum | solution.py:108
  311.6 6.4 copy.22
  317.9 5.7 all-to-all-start
  327.1 91.2 %all-gather.8.cloned.1.call-done = bf16[8192,256]{1,0:T(8,128)(2,1)} async-done(((bf16[512,256]{1,0:T(8,128)(2,1)}), bf16[8192,256]{1,0:T(8,128)(2,1)}) %all-gather.8.cloned.1.call-update) | async-done | bytes 4194320 | tf_op jit(solution)/shard_map/all_gather | solution.py:115
  418.3 6.5 all-to-all-done
  424.8 4.8 convolution_convert_fusion.1
  430.9 5.0 psum.36
  436.5 97.8 %all-reduce.11.cloned.1.call-done = f32[256,256]{0,1:T(8,128)} async-done(((f32[256,256]{0,1:T(8,128)}), f32[256,256]{0,1:T(8,128)}) %all-reduce.11.cloned.1.call-update) | async-done | bytes 262160 | tf_op jit(solution)/shard_map/psum | solution.py:120
  536.5 11.7 %cholesky.50 = f32[128,128]{1,0:T(8,128)S(1)} custom-call(f32[128,128]{1,0:T(8,128)S(1)} %cholesky.118), custom_call_target="Cholesky" | custom-call | tf_op jit(solution)/shard_map/jit(cholesky)/cholesky | solution.py:121
  548.3 9.8 %custom-call.15 = f32[1,128,128]{1,2,0:T(8,128)S(1)} custom-call(f32[1,128,128]{2,1,0:T(8,128)S(1)} %get-tuple-element.89), custom_call_target="InvertDiagBlocksLowerTriangular" | custom-call | tf_op jit(solution)/shard_map/jit(cholesky)/cholesky | solution.py:121
  558.5 11.7 %cholesky.105 = f32[128,128]{1,0:T(8,128)S(1)} custom-call(f32[128,128]{1,0:T(8,128)S(1)} %convolution_subtract_fusion.1), custom_call_target="Cholesky" | custom-call | tf_op jit(solution)/shard_map/jit(cholesky)/cholesky | solution.py:121
  573.0 5.3 while.1
  573.7 2.0 bitcast_dynamic-update-slice_fusion.2
  576.3 2.0 bitcast_dynamic-update-slice_fusion.2
  578.3 20.5 %custom-call.16 = f32[2,128,128]{1,2,0:T(8,128)S(1)} custom-call(f32[2,128,128]{2,1,0:T(8,128)} %get-tuple-element.11), custom_call_target="InvertDiagBlocksLowerTriangular" | custom-call | tf_op jit(solution)/shard_map/jit(_solve_triangular)/triangular_solve | solution.py:122
  600.4 3.9 collective-permute-start
  604.3 3.9 fusion.15
  610.4 4.4 collective-permute-start.2
  618.7 4.5 collective-permute-start.4
  625.7 4.7 collective-permute-start.6
  632.9 4.7 collective-permute-start.8
  640.1 4.7 collective-permute-start.10
  647.3 4.7 collective-permute-start.12
  654.7 5.7 collective-permute-done.14
  660.7 29.5 %psum.39 = f32[256]{0:T(256)S(1)} all-reduce(f32[256]{0:T(256)S(1)} %get-tuple-element.125), channel_id=1, replica_groups=mesh['dp'=2,'fsdp'=16] {'fsdp'}, use_global_device_ids=true, to_apply=%region_43.44 | all-reduce | flops 256 | bytes 2048 | tf_op jit(solution)/shard_map/psum | solution.py:157
  (224 shorter events, 43.3 us)
Async XLA Ops:
  7.2 1.1 copy-start
  7.2 82.5 %all-gather.4.cloned.1.call-start = ((), (), s32[]{:S(2)}) async-start(), calls=%async_computation.2 | async-start | bytes 3342336 | tf_op jit(solution)/shard_map/all_gather | solution.py:62
  45.0 5.6 copy-start.4
  45.0 6.6 copy-start.5
  45.1 112.9 %reduce-scatter.2.cloned.1.call-start = ((), (), s32[]{:S(2)}) async-start(), calls=%async_computation.4 | async-start | bytes 3342336 | tf_op jit(solution)/shard_map/reduce_scatter | solution.py:83
  50.5 149.2 %all-gather.6.cloned.1.call-start = ((), (), s32[]{:S(2)}) async-start(), calls=%async_computation.3 | async-start | bytes 1671168 | tf_op jit(solution)/shard_map/all_gather | solution.py:76
  99.5 100.2 %copy-start.3 = (bf16[1,192,512]{2,1,0:T(8,128)(2,1)S(1)}, bf16[1,192,512]{2,1,0:T(8,128)(2,1)}, u32[]{:S(2)}) copy-start(bf16[1,192,512]{2,1,0:T(8,128)(2,1)} %param.16) | copy-start | bytes 589828
  161.6 150.0 %all-reduce.9.cloned.1.call-start = ((), (), s32[]{:S(2)}) async-start(), calls=%async_computation.5 | async-start | bytes 8388608 | tf_op jit(solution)/shard_map/psum | solution.py:108
  204.4 213.9 %all-gather.8.cloned.1.call-start = ((), (), s32[]{:S(2)}) async-start(), calls=%async_computation.6 | async-start | bytes 4456448 | tf_op jit(solution)/shard_map/all_gather | solution.py:115
  317.9 106.8 %all-to-all-start = ((bf16[16,256,512]{1,2,0:T(8,128)(2,1)}), bf16[16,256,512]{1,2,0:T(8,128)(2,1)}, u32[]{:S(2)}, u32[]{:S(2)}) async-start(bf16[16,256,512]{1,2,0:T(8,128)(2,1)} %copy.22), calls=%async_computation.1 | async-start | bytes 8388608 | tf_op jit(solution)/shard_map/all_to_all | solution.py:112
  323.6 210.8 %all-reduce.11.cloned.1.call-start = ((), (), s32[]{:S(2)}) async-start(), calls=%async_computation.7 | async-start | bytes 524288 | tf_op jit(solution)/shard_map/psum | solution.py:120
  429.6 174.7 %copy-start.2 = (bf16[192,4096]{1,0:T(8,128)(2,1)S(1)}, bf16[192,4096]{1,0:T(8,128)(2,1)}, u32[]{:S(2)}) copy-start(bf16[192,4096]{1,0:T(8,128)(2,1)} %all-gather.6.cloned.1.call-done) | copy-start | bytes 4718596
  599.8 10.5 %collective-permute-start.1 = (bf16[256,256]{0,1:T(8,128)(2,1)S(1)}, bf16[256,256]{0,1:T(8,128)(2,1)S(1)}, u32[]{:S(2)}, u32[]{:S(2)}) collective-permute-start(bf16[256,256]{0,1:T(8,128)(2,1)S(1)} %fusion.73), channel_id=1, source_target_pairs={{0,1},{1,2},{2,3},{3,4},{4,5},{5,6},{6,7},{7,8},{8,9},{9,10},{10,1... | collective-permute-start | bytes 393224 | tf_op jit(solution)/shard_map/ppermute | solution.py:138
  600.4 10.0 %collective-permute-start = (bf16[256,256]{0,1:T(8,128)(2,1)S(1)}, bf16[256,256]{0,1:T(8,128)(2,1)S(1)}, u32[]{:S(2)}, u32[]{:S(2)}) collective-permute-start(bf16[256,256]{0,1:T(8,128)(2,1)S(1)} %fusion.73), channel_id=1, source_target_pairs={{0,15},{1,0},{2,1},{3,2},{4,3},{5,4},{6,5},{7,6},{8,7},{9,8},{10,9... | collective-permute-start | bytes 393224 | tf_op jit(solution)/shard_map/ppermute | solution.py:140
  608.9 14.2 %copy-start.1 = (bf16[4096,512]{1,0:T(8,128)(2,1)S(1)}, bf16[4096,512]{1,0:T(8,128)(2,1)}, u32[]{:S(2)}) copy-start(bf16[4096,512]{1,0:T(8,128)(2,1)} %all-reduce.9.cloned.1.call-done) | copy-start | bytes 12582916
  610.3 7.1 %collective-permute-start.3 = (bf16[256,256]{0,1:T(8,128)(2,1)S(1)}, bf16[256,256]{0,1:T(8,128)(2,1)S(1)}, u32[]{:S(2)}, u32[]{:S(2)}) collective-permute-start(bf16[256,256]{0,1:T(8,128)(2,1)S(1)} %collective-permute-done.1), channel_id=1, source_target_pairs={{0,1},{1,2},{2,3},{3,4},{4,5},{5,6},{6,7},{7,8},{8,9},{9,10},{10,1... | collective-permute-start | bytes 393224 | tf_op jit(solution)/shard_map/ppermute | solution.py:138
  610.4 8.3 %collective-permute-start.2 = (bf16[256,256]{0,1:T(8,128)(2,1)S(1)}, bf16[256,256]{0,1:T(8,128)(2,1)S(1)}, u32[]{:S(2)}, u32[]{:S(2)}) collective-permute-start(bf16[256,256]{0,1:T(8,128)(2,1)S(1)} %collective-permute-done), channel_id=1, source_target_pairs={{0,15},{1,0},{2,1},{3,2},{4,3},{5,4},{6,5},{7,6},{8,7},{9,8},{10,9... | collective-permute-start | bytes 393224 | tf_op jit(solution)/shard_map/ppermute | solution.py:140
  617.4 7.2 %collective-permute-start.5 = (bf16[256,256]{0,1:T(8,128)(2,1)S(1)}, bf16[256,256]{0,1:T(8,128)(2,1)S(1)}, u32[]{:S(2)}, u32[]{:S(2)}) collective-permute-start(bf16[256,256]{0,1:T(8,128)(2,1)S(1)} %collective-permute-done.3), channel_id=1, source_target_pairs={{0,1},{1,2},{2,3},{3,4},{4,5},{5,6},{6,7},{7,8},{8,9},{9,10},{10,1... | collective-permute-start | bytes 393224 | tf_op jit(solution)/shard_map/ppermute | solution.py:138
  618.7 7.0 %collective-permute-start.4 = (bf16[256,256]{0,1:T(8,128)(2,1)S(1)}, bf16[256,256]{0,1:T(8,128)(2,1)S(1)}, u32[]{:S(2)}, u32[]{:S(2)}) collective-permute-start(bf16[256,256]{0,1:T(8,128)(2,1)S(1)} %collective-permute-done.2), channel_id=1, source_target_pairs={{0,15},{1,0},{2,1},{3,2},{4,3},{5,4},{6,5},{7,6},{8,7},{9,8},{10,9... | collective-permute-start | bytes 393224 | tf_op jit(solution)/shard_map/ppermute | solution.py:140
  624.6 7.2 %collective-permute-start.7 = (bf16[256,256]{0,1:T(8,128)(2,1)S(1)}, bf16[256,256]{0,1:T(8,128)(2,1)S(1)}, u32[]{:S(2)}, u32[]{:S(2)}) collective-permute-start(bf16[256,256]{0,1:T(8,128)(2,1)S(1)} %collective-permute-done.5), channel_id=1, source_target_pairs={{0,1},{1,2},{2,3},{3,4},{4,5},{5,6},{6,7},{7,8},{8,9},{9,10},{10,1... | collective-permute-start | bytes 393224 | tf_op jit(solution)/shard_map/ppermute | solution.py:138
  625.7 7.2 %collective-permute-start.6 = (bf16[256,256]{0,1:T(8,128)(2,1)S(1)}, bf16[256,256]{0,1:T(8,128)(2,1)S(1)}, u32[]{:S(2)}, u32[]{:S(2)}) collective-permute-start(bf16[256,256]{0,1:T(8,128)(2,1)S(1)} %collective-permute-done.4), channel_id=1, source_target_pairs={{0,15},{1,0},{2,1},{3,2},{4,3},{5,4},{6,5},{7,6},{8,7},{9,8},{10,9... | collective-permute-start | bytes 393224 | tf_op jit(solution)/shard_map/ppermute | solution.py:140
  631.8 7.2 %collective-permute-start.9 = (bf16[256,256]{0,1:T(8,128)(2,1)S(1)}, bf16[256,256]{0,1:T(8,128)(2,1)S(1)}, u32[]{:S(2)}, u32[]{:S(2)}) collective-permute-start(bf16[256,256]{0,1:T(8,128)(2,1)S(1)} %collective-permute-done.7), channel_id=1, source_target_pairs={{0,1},{1,2},{2,3},{3,4},{4,5},{5,6},{6,7},{7,8},{8,9},{9,10},{10,1... | collective-permute-start | bytes 393224 | tf_op jit(solution)/shard_map/ppermute | solution.py:138
  632.9 7.2 %collective-permute-start.8 = (bf16[256,256]{0,1:T(8,128)(2,1)S(1)}, bf16[256,256]{0,1:T(8,128)(2,1)S(1)}, u32[]{:S(2)}, u32[]{:S(2)}) collective-permute-start(bf16[256,256]{0,1:T(8,128)(2,1)S(1)} %collective-permute-done.6), channel_id=1, source_target_pairs={{0,15},{1,0},{2,1},{3,2},{4,3},{5,4},{6,5},{7,6},{8,7},{9,8},{10,9... | collective-permute-start | bytes 393224 | tf_op jit(solution)/shard_map/ppermute | solution.py:140
  639.0 7.2 %collective-permute-start.11 = (bf16[256,256]{0,1:T(8,128)(2,1)S(1)}, bf16[256,256]{0,1:T(8,128)(2,1)S(1)}, u32[]{:S(2)}, u32[]{:S(2)}) collective-permute-start(bf16[256,256]{0,1:T(8,128)(2,1)S(1)} %collective-permute-done.9), channel_id=1, source_target_pairs={{0,1},{1,2},{2,3},{3,4},{4,5},{5,6},{6,7},{7,8},{8,9},{9,10},{10,1... | collective-permute-start | bytes 393224 | tf_op jit(solution)/shard_map/ppermute | solution.py:138
  640.1 7.2 %collective-permute-start.10 = (bf16[256,256]{0,1:T(8,128)(2,1)S(1)}, bf16[256,256]{0,1:T(8,128)(2,1)S(1)}, u32[]{:S(2)}, u32[]{:S(2)}) collective-permute-start(bf16[256,256]{0,1:T(8,128)(2,1)S(1)} %collective-permute-done.8), channel_id=1, source_target_pairs={{0,15},{1,0},{2,1},{3,2},{4,3},{5,4},{6,5},{7,6},{8,7},{9,8},{10,9... | collective-permute-start | bytes 393224 | tf_op jit(solution)/shard_map/ppermute | solution.py:140
  646.2 7.1 %collective-permute-start.13 = (bf16[256,256]{0,1:T(8,128)(2,1)S(1)}, bf16[256,256]{0,1:T(8,128)(2,1)S(1)}, u32[]{:S(2)}, u32[]{:S(2)}) collective-permute-start(bf16[256,256]{0,1:T(8,128)(2,1)S(1)} %collective-permute-done.11), channel_id=1, source_target_pairs={{0,1},{1,2},{2,3},{3,4},{4,5},{5,6},{6,7},{7,8},{8,9},{9,10},{10,1... | collective-permute-start | bytes 393224 | tf_op jit(solution)/shard_map/ppermute | solution.py:138
  647.3 7.2 %collective-permute-start.12 = (bf16[256,256]{0,1:T(8,128)(2,1)S(1)}, bf16[256,256]{0,1:T(8,128)(2,1)S(1)}, u32[]{:S(2)}, u32[]{:S(2)}) collective-permute-start(bf16[256,256]{0,1:T(8,128)(2,1)S(1)} %collective-permute-done.10), channel_id=1, source_target_pairs={{0,15},{1,0},{2,1},{3,2},{4,3},{5,4},{6,5},{7,6},{8,7},{9,8},{10,9... | collective-permute-start | bytes 393224 | tf_op jit(solution)/shard_map/ppermute | solution.py:140
  653.3 7.1 %collective-permute-start.14 = (bf16[256,256]{0,1:T(8,128)(2,1)S(1)}, bf16[256,256]{0,1:T(8,128)(2,1)S(1)}, u32[]{:S(2)}, u32[]{:S(2)}) collective-permute-start(bf16[256,256]{0,1:T(8,128)(2,1)S(1)} %collective-permute-done.13), channel_id=1, source_target_pairs={{0,1},{1,2},{2,3},{3,4},{4,5},{5,6},{6,7},{7,8},{8,9},{9,10},{10,1... | collective-permute-start | bytes 393224 | tf_op jit(solution)/shard_map/ppermute | solution.py:138
Sparse Core Ops, SparseCore 0:
  45.2 44.4 all-gather.3
  93.5 64.4 reduce-scatter.1
  161.7 37.9 all-gather.5
  204.5 106.9 all-reduce.8
  313.8 104.4 all-gather.7
  430.6 103.7 all-reduce.10
